TPU v7x, 32 devices: a whole 2x2x4 slice. The times are simulated.
32 devices in a mesh: group: 2 (over x), wide: 16 (over z, y, core).
Axes of the slice: x: 2, y: 2, z: 4, core: 2. Of those that a mesh axis runs over, the one named last changes fastest.
Arguments:
- tokens: bfloat16 [192, 2688], P('group', 'wide'), parts along dimension 0, may hold values from -6 to 6
- mix_gain: bfloat16 [2688], replicated, may hold values from 0.099609375 to 1.8984375
- proj_inner: bfloat16 [2688, 2, 4096], P(None, None, 'wide'), may hold values from -0.125 to 0.125
- proj_maps: bfloat16 [2688, 2048], P(None, 'wide'), may hold values from -0.125 to 0.125
- proj_step: bfloat16 [2688, 64], P(None, 'wide'), may hold values from -0.125 to 0.125
- window_inner: bfloat16 [192, 3, 4096], P('group', None, 'wide'), parts along dimension 0, may hold values from -6 to 6
- window_maps: bfloat16 [192, 3, 2048], P('group', None, 'wide'), parts along dimension 0, may hold values from -6 to 6
- kernel_inner: bfloat16 [4, 4096], P(None, 'wide'), may hold values from -3 to 3
- kernel_maps: bfloat16 [4, 2048], P(None, 'wide'), may hold values from -3 to 3
- step_bias: float32 [64], P('wide'), may hold values from -4 to -1
- decay_log: float32 [64], P('wide'), may hold values from -1 to 2.5
- skip_gain: float32 [64], P('wide'), may hold values from 0.5 to 2
- gated_gain: bfloat16 [4096], P('wide'), may hold values from 0.099609375 to 1.8984375
- proj_out: bfloat16 [4096, 2688], P('wide'), may hold values from -0.125 to 0.125
- ssm_state: float32 [192, 64, 64, 128], P('group', 'wide'), parts along dimension 0, may hold values from -0.6 to 0.6
- moe_gain: bfloat16 [2688], replicated, may hold values from 0.099609375 to 1.8984375
- router_weight: bfloat16 [2688, 16], replicated, may hold values from -0.125 to 0.125
- expert_ids: int32 [192, 6], P('group'), parts along dimension 0, may hold values from 0 to 15, all different within a row; in each aligned block of 96 rows (0 to 95, 96 to 191, ...) at most 96 rows name the same one
- expert_up: bfloat16 [16, 2688, 928], P('wide'), may hold values from -0.125 to 0.125
- expert_down: bfloat16 [16, 928, 2688], P('wide'), may hold values from -0.1875 to 0.1875
Outputs:
- next_hidden: bfloat16 [192, 2688], P('group', 'wide'), parts along dimension 0
- new_state: float32 [192, 64, 64, 128], P('group', 'wide'), parts along dimension 0
There are 2 independent parts, one for each index of `group`. A program takes and returns all parts, laid end to end along the dimension named above; an argument that names none is the same for every part. Nothing has to cross between parts.
Inputs may be any that keep to these rules, and one draw needn't show every extreme that they name: `expert_ids`: each token names 6 different experts; no expert is named by more than 96 tokens of a part, a bound that some block reaches.
All inputs are finite; a program needn't handle non-finite values.
Results may differ from a plain program's by a relative error of at most 0.013.
Values may be sent and summed in bfloat16 or wider, within the bound.
A program may use at most 128 MiB of HBM per device.

v0:
```python
import jax
import jax.numpy as jnp
from jax import lax
from jax.sharding import PartitionSpec as P

WIDTH = 2688
HEADS = 64
HEAD_DIM = 64
STATE = 128
GROUPS = 8
TOPK = 6
INNER = 4096
epsilon = 1e-05


def rms_scale(values, axis):
    return lax.rsqrt(jnp.mean(values * values, axis=axis, keepdims=True) + epsilon)


def convolve(window, fresh, kernel):
    stacked = jnp.concatenate([window, fresh[:, None, :]], axis=1).astype(jnp.float32)
    mixed = jnp.sum(stacked * kernel.astype(jnp.float32)[None], axis=1)
    return jax.nn.silu(mixed).astype(jnp.bfloat16)


def expert_rows(rows, upward, downward):
    hidden_units = jnp.dot(rows, upward, preferred_element_type=jnp.float32)
    active = jnp.square(jnp.maximum(hidden_units, 0.0)).astype(jnp.bfloat16)
    return jnp.dot(active, downward, preferred_element_type=jnp.float32).astype(jnp.bfloat16)


def route_gates(logits, expert_ids):
    onehot = (
        expert_ids[:, :, None] == jnp.arange(logits.shape[1], dtype=jnp.int32)[None, None, :]
    ).astype(jnp.float32)
    chosen = jnp.sum(onehot * logits[:, None, :], axis=2)
    score = jax.nn.sigmoid(chosen)
    return score / jnp.sum(score, axis=1, keepdims=True)


def slot_codes(expert_ids, experts, capacity):
    flat = expert_ids.reshape(-1)
    onehot = (flat[:, None] == jnp.arange(experts, dtype=jnp.int32)[None, :]).astype(jnp.int32)
    before = jnp.cumsum(onehot, axis=0) - onehot
    slots = jnp.sum(before * onehot, axis=1)
    return (flat * capacity + slots).reshape(expert_ids.shape)


def slot_tables(codes, gates, count):
    targets = jnp.arange(count, dtype=jnp.int32)
    match = codes[None, :, :] == targets[:, None, None]
    pick = jnp.any(match, axis=2).astype(jnp.bfloat16)
    weigh = jnp.sum(jnp.where(match, gates[None], 0.0), axis=2)
    return (pick, weigh)


def local(
    tokens,
    mix_gain,
    proj_inner,
    proj_maps,
    proj_step,
    window_inner,
    window_maps,
    kernel_inner,
    kernel_maps,
    step_bias,
    decay_log,
    skip_gain,
    gated_gain,
    proj_out,
    ssm_state,
    moe_gain,
    router_weight,
    expert_ids,
    expert_up,
    expert_down,
):
    devices = lax.axis_size("wide")
    device = lax.axis_index("wide")
    seqs = tokens.shape[0]
    slice_width = tokens.shape[1]
    capacity = min(seqs, 4 * seqs * TOPK // devices)
    full_tokens = lax.all_gather(tokens, "wide", axis=1, tiled=True)
    tokens_float = full_tokens.astype(jnp.float32)
    normed = (tokens_float * rms_scale(tokens_float, 1) * mix_gain.astype(jnp.float32)).astype(
        jnp.bfloat16
    )
    local_inner = proj_inner.shape[2]
    inner = jnp.dot(
        normed, proj_inner.reshape(WIDTH, 2 * local_inner), preferred_element_type=jnp.float32
    ).astype(jnp.bfloat16)
    gate_input = inner[:, :local_inner]
    raw_inner = inner[:, local_inner:]
    maps_raw = jnp.dot(normed, proj_maps, preferred_element_type=jnp.float32).astype(jnp.bfloat16)
    step_raw = jnp.dot(normed, proj_step, preferred_element_type=jnp.float32).astype(jnp.bfloat16)
    conv_inner = convolve(window_inner, raw_inner, kernel_inner)
    conv_maps = convolve(window_maps, maps_raw, kernel_maps)
    all_maps = lax.all_gather(conv_maps, "wide", axis=1, tiled=True)
    local_heads = proj_step.shape[1]
    group = device * local_heads // (HEADS // GROUPS)
    in_maps = lax.dynamic_slice_in_dim(all_maps, group * STATE, STATE, 1).astype(jnp.float32)
    out_maps = lax.dynamic_slice_in_dim(all_maps, GROUPS * STATE + group * STATE, STATE, 1).astype(
        jnp.float32
    )
    step_size = jax.nn.softplus(step_raw.astype(jnp.float32) + step_bias)
    decay = jnp.exp(-jnp.exp(decay_log) * step_size)
    head_inputs = conv_inner.astype(jnp.float32).reshape(seqs, local_heads, HEAD_DIM)
    driven = (step_size[:, :, None] * head_inputs)[..., None] * in_maps[:, None, None, :]
    new_state = decay[:, :, None, None] * ssm_state + driven
    readout = (
        jnp.einsum("shpn,sn->shp", new_state, out_maps, precision=lax.Precision.HIGHEST)
        + skip_gain[None, :, None] * head_inputs
    )
    gated = readout.reshape(seqs, local_inner) * jax.nn.silu(gate_input.astype(jnp.float32))
    group_mask = (jnp.arange(GROUPS, dtype=jnp.int32) == group).astype(jnp.float32)
    partial_squares = jnp.sum(gated * gated, axis=1)[:, None] * group_mask[None, :]
    group_squares = lax.psum(partial_squares, "wide")
    own_squares = jnp.sum(group_squares * group_mask[None, :], axis=1, keepdims=True)
    norm_scale = lax.rsqrt(own_squares / (INNER // GROUPS) + epsilon)
    gated_out = (gated * norm_scale * gated_gain.astype(jnp.float32)).astype(jnp.bfloat16)
    mixer_terms = jnp.dot(gated_out, proj_out, preferred_element_type=jnp.float32)
    codes = slot_codes(expert_ids, devices, capacity)
    mixer_slice = lax.psum_scatter(mixer_terms, "wide", scatter_dimension=1, tiled=True)
    hidden_round = (tokens.astype(jnp.float32) + mixer_slice).astype(jnp.bfloat16)
    hidden_slice = lax.optimization_barrier(hidden_round).astype(jnp.float32)
    gain_slice = lax.dynamic_slice_in_dim(moe_gain, device * slice_width, slice_width, 0).astype(
        jnp.float32
    )
    router_slice = lax.dynamic_slice_in_dim(
        router_weight, device * slice_width, slice_width, 0
    ).astype(jnp.float32)
    weighted = hidden_slice * gain_slice
    squares, part_logits = lax.psum(
        (
            jnp.sum(hidden_slice * hidden_slice, axis=1),
            jnp.dot(weighted, router_slice, precision=lax.Precision.HIGHEST),
        ),
        "wide",
    )
    moe_scale = lax.rsqrt(squares[:, None] / WIDTH + epsilon)
    gates = route_gates(part_logits * moe_scale, expert_ids)
    moe_input = (hidden_slice * moe_scale * gain_slice).astype(jnp.bfloat16)
    pick, weigh = slot_tables(codes, gates, devices * capacity)
    sent = (
        jnp.dot(pick, moe_input, preferred_element_type=jnp.float32)
        .astype(jnp.bfloat16)
        .reshape(devices, capacity, slice_width)
    )
    served = expert_rows(
        lax.all_to_all(sent, "wide", split_axis=0, concat_axis=2, tiled=True)[0],
        expert_up[0],
        expert_down[0],
    )
    returned = lax.all_to_all(served[None], "wide", split_axis=2, concat_axis=0, tiled=True)
    moe_slice = jnp.dot(
        weigh.T,
        returned.reshape(devices * capacity, slice_width).astype(jnp.float32),
        precision=lax.Precision.HIGHEST,
    )
    next_hidden = (hidden_slice + moe_slice).astype(jnp.bfloat16)
    return (next_hidden, new_state)


def solution(mesh):
    in_specs = (
        P("group", "wide"),
        P(),
        P(None, None, "wide"),
        P(None, "wide"),
        P(None, "wide"),
        P("group", None, "wide"),
        P("group", None, "wide"),
        P(None, "wide"),
        P(None, "wide"),
        P("wide"),
        P("wide"),
        P("wide"),
        P("wide"),
        P("wide", None),
        P("group", "wide", None, None),
        P(),
        P(),
        P("group", None),
        P("wide", None, None),
        P("wide", None, None),
    )
    out_specs = (P("group", "wide"), P("group", "wide", None, None))
    return jax.shard_map(local, mesh=mesh, in_specs=in_specs, out_specs=out_specs, check_vma=False)
```

profile of v0, /device:TPU:0, one launch (start us, length us, event | category | flops | bytes accessed | tf_op | source)
XLA Modules:
  0.0 292.7 jit_solution(6536486973410003831)
XLA Ops:
  7.3 25.6 %all_gather.6 = bf16[96,2688]{0,1:T(8,128)(2,1)S(1)} all-gather(bf16[96,168]{0,1:T(8,128)(2,1)} %param.20), channel_id=1, replica_groups=mesh['group'=2,'wide'=16] {'wide'}, dimensions={1}, use_global_device_ids=true | all-gather | bytes 548352 | tf_op jit(solution)/shard_map/all_gather | solution.py:84
  34.6 1.8 fusion.24
  36.6 18.5 %all_gather.7 = bf16[96,2048]{1,0:T(8,128)(2,1)S(1)} all-gather(bf16[96,128]{1,0:T(8,128)(2,1)S(1)} %multiply_convert_fusion.3), channel_id=1, replica_groups=mesh['group'=2,'wide'=16] {'wide'}, dimensions={1}, use_global_device_ids=true | all-gather | bytes 417792 | tf_op jit(solution)/shard_map/all_gather | solution.py:99
  55.6 1.2 convolution_convert_fusion.1
  57.9 7.0 %multiply_add_fusion = f32[96,4,64,128]{3,2,1,0:T(8,128)S(1)} fusion(f32[96,4,64,128]{3,2,1,0:T(8,128)} %param.34, f32[96,128]{1,0:T(8,128)S(1)} %get-tuple-element.5, f32[96,4,64]{2,1,0:T(4,128)S(1)} %copy.72, f32[96,4]{1,0:T(8,128)S(1)} %copy.70), kind=kLoop, calls=%fused_computation | loop fusion | flops 9437184 | bytes 25314816 | tf_op jit(solution)/shard_map/add | solution.py:110
  64.9 4.8 %copy-done.1 = f32[96,4,64,128]{3,2,1,0:T(8,128)} copy-done((f32[96,4,64,128]{3,2,1,0:T(8,128)}, f32[96,4,64,128]{3,2,1,0:T(8,128)S(1)}, u32[]{:S(2)}) %copy-start.1) | copy-done | bytes 12582936
  69.7 14.7 %fusion.40 = f32[96,1,4,64]{3,1,2,0:T(1,128)S(1)} fusion(f32[96,4,64,128]{3,2,1,0:T(8,128)S(1)} %multiply_add_fusion, bf16[96,128,1,1]{1,0,2,3:T(8,128)(2,1)S(1)} %get-tuple-element.4), kind=kOutput, calls=%fused_computation.52 | convolution fusion | flops 37748736 | bytes 12705792 | tf_op jit(solution)/shard_map/shpn,sn->shp/dot_general | solution.py:112
  84.9 31.1 %psum.21 = f32[96,8]{0,1:T(8,128)S(1)} all-reduce(f32[96,8]{0,1:T(8,128)S(1)} %broadcast_multiply_fusion.1), channel_id=1, replica_groups=mesh['group'=2,'wide'=16] {'wide'}, use_global_device_ids=true, to_apply=%region_4.5 | all-reduce | flops 768 | bytes 6144 | tf_op jit(solution)/shard_map/psum | solution.py:118
  116.1 1.8 fusion.39
  118.2 1.7 reduce-window.6
  121.9 50.8 %reduce-scatter.4.cloned.1.call-done = f32[96,168]{0,1:T(8,128)} async-done(((f32[96,2688]{0,1:T(8,128)}), f32[96,168]{0,1:T(8,128)}) %reduce-scatter.4.cloned.1.call-update) | async-done | bytes 64528
  174.5 30.5 %all-reduce.2 = (f32[96,16]{0,1:T(8,128)S(1)}, f32[96]{0:T(128)S(1)}) all-reduce(f32[96,16]{0,1:T(8,128)S(1)} %fusion.35, f32[96]{0:T(128)S(1)} %fusion.36), channel_id=1, replica_groups=mesh['group'=2,'wide'=16] {'wide'}, use_global_device_ids=true, to_apply=%region_10.11 | all-reduce | flops 1632 | bytes 13056 | tf_op jit(solution)/shard_map/psum | solution.py:134
  206.1 21.2 %all_to_all.30 = bf16[16,96,168]{1,2,0:T(8,128)(2,1)S(1)} all-to-all(bf16[16,96,168]{1,2,0:T(8,128)(2,1)S(1)} %copy.78), channel_id=1, replica_groups=mesh['group'=2,'wide'=16] {'wide'}, dimensions={0} | all-to-all | bytes 1032192 | tf_op jit(solution)/shard_map/all_to_all | solution.py:151
  227.4 6.5 %fusion.8 = bf16[1,96,2688]{2,1,0:T(8,128)(2,1)S(1)} fusion(bf16[1,928,2688]{2,1,0:T(8,128)(2,1)} %param.39, bf16[96,2688]{0,1:T(8,128)(2,1)S(1)} %bitcast.74, bf16[1,2688,928]{1,2,0:T(8,128)(2,1)} %param.38), kind=kOutput, calls=%fused_computation.9 | convolution fusion | flops 958399488 | bytes 11010048 | tf_op jit(solution)/shard_map/dot_general | solution.py:29
  233.9 1.9 copy.80
  236.3 14.9 %reduce.2 = bf16[2688,96]{1,0:T(8,128)(2,1)S(1)} reduce(bf16[2688,1,96]{2,1,0:T(2,128)(2,1)S(1)} %bitcast.70, bf16[]{:T(256)} %broadcast.123), dimensions={1}, to_apply=%bitcast.55.reduce_sub_computation | reduce | bytes 1032194
  251.3 1.9 reshape.122
  253.2 4.5 %all-to-all-start.1 = ((bf16[16,2,8064]{2,1,0:T(2,128)(2,1)}), bf16[16,2,8064]{2,1,0:T(2,128)(2,1)}, u32[]{:S(2)}, u32[]{:S(2)}) async-start(bf16[16,2,8064]{2,1,0:T(2,128)(2,1)} %reshape.122), calls=%async_computation.1 | async-start | bytes 1032192 | tf_op jit(solution)/shard_map/all_to_all | solution.py:155
  258.3 13.3 %all-to-all-done.1 = bf16[16,2,8064]{2,1,0:T(2,128)(2,1)} async-done(((bf16[16,2,8064]{2,1,0:T(2,128)(2,1)}), bf16[16,2,8064]{2,1,0:T(2,128)(2,1)}, u32[]{:S(2)}, u32[]{:S(2)}) %all-to-all-start.1) | async-done | bytes 516128 | tf_op jit(solution)/shard_map/all_to_all | solution.py:155
  271.6 5.0 %reshape.123 = bf16[2688,1,96]{2,1,0:T(2,128)(2,1)S(1)} reshape(bf16[16,2,8064]{2,1,0:T(2,128)(2,1)} %all-to-all-done.1) | data formatting | bytes 1032192
  276.6 2.8 copy.81
  279.4 3.3 %all_to_all.26 = bf16[1,96,16,168]{3,2,1,0:T(8,128)(2,1)S(1)} reshape(bf16[1,96,2688]{2,1,0:T(8,128)(2,1)} %copy.81) | data formatting | bytes 1032192 | tf_op jit(solution)/shard_map/all_to_all | solution.py:155
  282.7 1.2 copy.82
  284.6 1.2 fusion.23
  (80 shorter events, 11.0 us)
Async XLA Ops:
  7.2 108.9 %copy-start = (bf16[256,2688]{1,0:T(8,128)(2,1)S(1)}, bf16[256,2688]{1,0:T(8,128)(2,1)}, u32[]{:S(2)}) copy-start(bf16[256,2688]{1,0:T(8,128)(2,1)} %param.33) | copy-start | bytes 4128772
  7.2 29.3 %copy-start.5 = (bf16[96,3,128]{2,0,1:T(8,128)(2,1)S(1)}, bf16[96,3,128]{2,0,1:T(8,128)(2,1)}, u32[]{:S(2)}) copy-start(bf16[96,3,128]{2,0,1:T(8,128)(2,1)} %param.26) | copy-start | bytes 221188
  7.2 165.5 %reduce-scatter.4.cloned.1.call-start = ((), (), s32[]{:S(2)}) async-start(), calls=%async_computation.3 | async-start | bytes 1462272
  7.3 47.8 %copy-start.2 = (bf16[2688,2,256]{2,1,0:T(2,128)(2,1)S(1)}, bf16[2688,2,256]{2,1,0:T(2,128)(2,1)}, u32[]{:S(2)}) copy-start(bf16[2688,2,256]{2,1,0:T(2,128)(2,1)} %param.22) | copy-start | bytes 8257540
  55.5 1.3 copy-start.7
  55.6 1.3 copy-start.4
  55.6 1.4 copy-start.10
  55.6 1.4 copy-start.9
  55.6 1.4 copy-start.11
  64.9 4.8 %copy-start.1 = (f32[96,4,64,128]{3,2,1,0:T(8,128)}, f32[96,4,64,128]{3,2,1,0:T(8,128)S(1)}, u32[]{:S(2)}) copy-start(f32[96,4,64,128]{3,2,1,0:T(8,128)S(1)} %multiply_add_fusion) | copy-start | bytes 37748740
  69.7 14.8 %copy-start.8 = (f32[4]{0:T(128)S(1)}, f32[4]{0:T(128)}, u32[]{:S(2)}) copy-start(f32[4]{0:T(128)} %param.31) | copy-start | bytes 52
  69.7 46.4 %copy-start.12 = (bf16[256]{0:T(256)(128)(2,1)S(1)}, bf16[256]{0:T(256)(128)(2,1)}, u32[]{:S(2)}) copy-start(bf16[256]{0:T(256)(128)(2,1)} %param.32) | copy-start | bytes 1540
  84.4 33.6 %copy-start.6 = (s32[96,6]{0,1:T(8,128)S(1)}, s32[96,6]{0,1:T(8,128)}, u32[]{:S(2)}) copy-start(s32[96,6]{0,1:T(8,128)} %param.37) | copy-start | bytes 6916
  84.6 88.1 %copy-start.3 = (bf16[96,168]{0,1:T(8,128)(2,1)S(1)}, bf16[96,168]{0,1:T(8,128)(2,1)}, u32[]{:S(2)}) copy-start(bf16[96,168]{0,1:T(8,128)(2,1)} %param.20) | copy-start | bytes 96772
  253.2 18.4 %all-to-all-start.1 = ((bf16[16,2,8064]{2,1,0:T(2,128)(2,1)}), bf16[16,2,8064]{2,1,0:T(2,128)(2,1)}, u32[]{:S(2)}, u32[]{:S(2)}) async-start(bf16[16,2,8064]{2,1,0:T(2,128)(2,1)} %reshape.122), calls=%async_computation.1 | async-start | bytes 1032192 | tf_op jit(solution)/shard_map/all_to_all | solution.py:155
Sparse Core Ops, SparseCore 0:
  118.0 54.5 reduce-scatter.3
where the time goes:
time: 293 us
  blocking collectives  127 us (43%)
  waiting for transfers between devices  64.1 us (22%)
  other arithmetic  29 us (10%)
  matrix products  29 us (10%)
  local copies, waits for them, and re-layouts  24.6 us (8%)
  between operations  14.5 us (5%)
  starting transfers between devices  4.53 us (2%)
    unnamed x2, waiting for transfers between devices  50.8 us
    psum x1, blocking collectives, local(): group_squares = lax.psum(partial_squares, 'wide')  31.1 us
    psum x1, blocking collectives, local(): lax.psum((jnp.sum(hidden_slice * hidden_slice, axis=1), jnp.dot(weighted,...  30.5 us
    all_gather x1, blocking collectives, local(): full_tokens = lax.all_gather(tokens, 'wide', axis=1, tiled=True)  25.6 us
    all_to_all x1, blocking collectives, local(): lax.all_to_all(sent, 'wide', split_axis=0, concat_axis=2, tiled=True)[0]  21.2 us
    all_gather x1, blocking collectives, local(): all_maps = lax.all_gather(conv_maps, 'wide', axis=1, tiled=True)  18.5 us
    unnamed x1, other arithmetic  14.9 us
    dot_general x1, matrix products, local(): jnp.einsum('shpn,sn->shp', new_state, out_maps, precision=lax.Precision.H...  14.7 us
  transfers between devices with their start and end apart: 2, of which 2 were waited for; matrix products, arithmetic and copies ran while one was open for 2% of the time, Pallas kernels for 0%

commit v1 on v0

--- a/solution.py
+++ b/solution.py
@@ -81,7 +81,7 @@
     seqs = tokens.shape[0]
     slice_width = tokens.shape[1]
     capacity = min(seqs, 4 * seqs * TOPK // devices)
-    full_tokens = lax.all_gather(tokens, "wide", axis=1, tiled=True)
+    full_tokens = jnp.concatenate(lax.all_gather(tokens, "wide"), axis=1)
     tokens_float = full_tokens.astype(jnp.float32)
     normed = (tokens_float * rms_scale(tokens_float, 1) * mix_gain.astype(jnp.float32)).astype(
         jnp.bfloat16

time: 293 us -> 294 us (level)
  no operation moved by 1% of the time
where the time goes in v1:
time: 294 us; the launch traced here: 293 us
  blocking collectives  127 us (43%)
  waiting for transfers between devices  64.1 us (22%)
  other arithmetic  29.9 us (10%)
  matrix products  27.8 us (9%)
  local copies, waits for them, and re-layouts  25.4 us (9%)
  between operations  14.6 us (5%)
  starting transfers between devices  4.53 us (2%)
    unnamed x2, waiting for transfers between devices  50.8 us
    psum x1, blocking collectives, local(): group_squares = lax.psum(partial_squares, 'wide')  31.1 us
    psum x1, blocking collectives, local(): lax.psum((jnp.sum(hidden_slice * hidden_slice, axis=1), jnp.dot(weighted,...  30.5 us
    all_gather x1, blocking collectives, local(): full_tokens = jnp.concatenate(lax.all_gather(tokens, 'wide'), axis=1)  25.6 us
    all_to_all x1, blocking collectives, local(): lax.all_to_all(sent, 'wide', split_axis=0, concat_axis=2, tiled=True)[0]  21.2 us
    all_gather x1, blocking collectives, local(): all_maps = lax.all_gather(conv_maps, 'wide', axis=1, tiled=True)  18.5 us
    unnamed x1, other arithmetic  14.9 us
    dot_general x1, matrix products, local(): jnp.einsum('shpn,sn->shp', new_state, out_maps, precision=lax.Precision.H...  14.7 us
  transfers between devices with their start and end apart: 2, of which 2 were waited for; matrix products, arithmetic and copies ran while one was open for 2% of the time, Pallas kernels for 0%

profile of v1, /device:TPU:0, one launch (start us, length us, event | category | flops | bytes accessed | tf_op | source)
XLA Modules:
  0.0 293.2 jit_solution(6500956882181372410)
XLA Ops:
  8.9 25.6 %all-gather.1 = bf16[16,96,168]{1,2,0:T(8,128)(2,1)S(1)} all-gather(bf16[1,96,168]{1,2,0:T(8,128)(2,1)} %bitcast.94), channel_id=2, replica_groups=mesh['group'=2,'wide'=16] {'wide'}, dimensions={0}, use_global_device_ids=true | all-gather | bytes 548352 | tf_op jit(solution)/shard_map/all_gather | solution.py:84
  36.0 1.5 fusion.23
  37.5 18.5 %all_gather.11 = bf16[96,2048]{1,0:T(8,128)(2,1)S(1)} all-gather(bf16[96,128]{1,0:T(8,128)(2,1)S(1)} %multiply_convert_fusion.4), channel_id=1, replica_groups=mesh['group'=2,'wide'=16] {'wide'}, dimensions={1}, use_global_device_ids=true | all-gather | bytes 417792 | tf_op jit(solution)/shard_map/all_gather | solution.py:99
  58.4 7.0 %multiply_add_fusion = f32[96,4,64,128]{3,2,1,0:T(8,128)S(1)} fusion(f32[96,4,64,128]{3,2,1,0:T(8,128)} %param.34, f32[96,128]{1,0:T(8,128)S(1)} %get-tuple-element.5, f32[96,4,64]{2,1,0:T(4,128)S(1)} %copy.72, f32[96,4]{1,0:T(8,128)S(1)} %copy.70), kind=kLoop, calls=%fused_computation | loop fusion | flops 9437184 | bytes 25314816 | tf_op jit(solution)/shard_map/add | solution.py:110
  65.4 4.8 %copy-done.1 = f32[96,4,64,128]{3,2,1,0:T(8,128)} copy-done((f32[96,4,64,128]{3,2,1,0:T(8,128)}, f32[96,4,64,128]{3,2,1,0:T(8,128)S(1)}, u32[]{:S(2)}) %copy-start.1) | copy-done | bytes 12582936
  70.2 14.7 %fusion.39 = f32[96,1,4,64]{3,1,2,0:T(1,128)S(1)} fusion(f32[96,4,64,128]{3,2,1,0:T(8,128)S(1)} %multiply_add_fusion, bf16[96,128,1,1]{1,0,2,3:T(8,128)(2,1)S(1)} %get-tuple-element.4), kind=kOutput, calls=%fused_computation.52 | convolution fusion | flops 37748736 | bytes 12705792 | tf_op jit(solution)/shard_map/shpn,sn->shp/dot_general | solution.py:112
  85.4 31.1 %psum.21 = f32[96,8]{0,1:T(8,128)S(1)} all-reduce(f32[96,8]{0,1:T(8,128)S(1)} %broadcast_multiply_fusion.1), channel_id=1, replica_groups=mesh['group'=2,'wide'=16] {'wide'}, use_global_device_ids=true, to_apply=%region_4.5 | all-reduce | flops 768 | bytes 6144 | tf_op jit(solution)/shard_map/psum | solution.py:118
  116.6 1.8 fusion.38
  118.7 1.7 reduce-window.6
  122.3 50.8 %reduce-scatter.4.cloned.1.call-done = f32[96,168]{0,1:T(8,128)} async-done(((f32[96,2688]{0,1:T(8,128)}), f32[96,168]{0,1:T(8,128)}) %reduce-scatter.4.cloned.1.call-update) | async-done | bytes 64528
  174.1 0.9 fusion.34
  175.0 30.5 %all-reduce.2 = (f32[96,16]{0,1:T(8,128)S(1)}, f32[96]{0:T(128)S(1)}) all-reduce(f32[96,16]{0,1:T(8,128)S(1)} %fusion.34, f32[96]{0:T(128)S(1)} %fusion.35), channel_id=1, replica_groups=mesh['group'=2,'wide'=16] {'wide'}, use_global_device_ids=true, to_apply=%region_10.11 | all-reduce | flops 1632 | bytes 13056 | tf_op jit(solution)/shard_map/psum | solution.py:134
  206.6 21.2 %all_to_all.30 = bf16[16,96,168]{1,2,0:T(8,128)(2,1)S(1)} all-to-all(bf16[16,96,168]{1,2,0:T(8,128)(2,1)S(1)} %copy.78), channel_id=1, replica_groups=mesh['group'=2,'wide'=16] {'wide'}, dimensions={0} | all-to-all | bytes 1032192 | tf_op jit(solution)/shard_map/all_to_all | solution.py:151
  227.8 6.5 %fusion.8 = bf16[1,96,2688]{2,1,0:T(8,128)(2,1)S(1)} fusion(bf16[1,928,2688]{2,1,0:T(8,128)(2,1)} %param.39, bf16[96,2688]{0,1:T(8,128)(2,1)S(1)} %bitcast.90, bf16[1,2688,928]{1,2,0:T(8,128)(2,1)} %param.38), kind=kOutput, calls=%fused_computation.9 | convolution fusion | flops 958399488 | bytes 11010048 | tf_op jit(solution)/shard_map/dot_general | solution.py:29
  234.4 1.9 copy.80
  236.8 14.9 %reduce.4 = bf16[2688,96]{1,0:T(8,128)(2,1)S(1)} reduce(bf16[2688,1,96]{2,1,0:T(2,128)(2,1)S(1)} %bitcast.85, bf16[]{:T(256)} %broadcast.131), dimensions={1}, to_apply=%bitcast.67.reduce_sub_computation | reduce | bytes 1032194
  251.8 1.9 reshape.144
  253.7 4.5 %all-to-all-start.1 = ((bf16[16,2,8064]{2,1,0:T(2,128)(2,1)}), bf16[16,2,8064]{2,1,0:T(2,128)(2,1)}, u32[]{:S(2)}, u32[]{:S(2)}) async-start(bf16[16,2,8064]{2,1,0:T(2,128)(2,1)} %reshape.144), calls=%async_computation.1 | async-start | bytes 1032192 | tf_op jit(solution)/shard_map/all_to_all | solution.py:155
  258.8 13.3 %all-to-all-done.1 = bf16[16,2,8064]{2,1,0:T(2,128)(2,1)} async-done(((bf16[16,2,8064]{2,1,0:T(2,128)(2,1)}), bf16[16,2,8064]{2,1,0:T(2,128)(2,1)}, u32[]{:S(2)}, u32[]{:S(2)}) %all-to-all-start.1) | async-done | bytes 516128 | tf_op jit(solution)/shard_map/all_to_all | solution.py:155
  272.1 5.0 %reshape.145 = bf16[2688,1,96]{2,1,0:T(2,128)(2,1)S(1)} reshape(bf16[16,2,8064]{2,1,0:T(2,128)(2,1)} %all-to-all-done.1) | data formatting | bytes 1032192
  277.1 2.8 copy.81
  279.9 3.3 %all_to_all.26 = bf16[1,96,16,168]{3,2,1,0:T(8,128)(2,1)S(1)} reshape(bf16[1,96,2688]{2,1,0:T(8,128)(2,1)} %copy.81) | data formatting | bytes 1032192 | tf_op jit(solution)/shard_map/all_to_all | solution.py:155
  283.2 1.2 copy.82
  285.1 1.2 fusion.22
  (83 shorter events, 12.1 us)
Async XLA Ops:
  7.2 109.4 %copy-start = (bf16[256,2688]{1,0:T(8,128)(2,1)S(1)}, bf16[256,2688]{1,0:T(8,128)(2,1)}, u32[]{:S(2)}) copy-start(bf16[256,2688]{1,0:T(8,128)(2,1)} %param.33) | copy-start | bytes 4128772
  7.2 30.3 %copy-start.5 = (bf16[96,3,128]{2,0,1:T(8,128)(2,1)S(1)}, bf16[96,3,128]{2,0,1:T(8,128)(2,1)}, u32[]{:S(2)}) copy-start(bf16[96,3,128]{2,0,1:T(8,128)(2,1)} %param.26) | copy-start | bytes 221188
  7.2 165.9 %reduce-scatter.4.cloned.1.call-start = ((), (), s32[]{:S(2)}) async-start(), calls=%async_computation.3 | async-start | bytes 1462272
  8.9 47.6 %copy-start.2 = (bf16[2688,2,256]{2,1,0:T(2,128)(2,1)S(1)}, bf16[2688,2,256]{2,1,0:T(2,128)(2,1)}, u32[]{:S(2)}) copy-start(bf16[2688,2,256]{2,1,0:T(2,128)(2,1)} %param.22) | copy-start | bytes 8257540
  56.5 1.2 copy-start.7
  56.5 1.2 copy-start.4
  56.5 1.3 copy-start.10
  56.5 1.3 copy-start.9
  56.5 1.3 copy-start.11
  65.4 4.8 %copy-start.1 = (f32[96,4,64,128]{3,2,1,0:T(8,128)}, f32[96,4,64,128]{3,2,1,0:T(8,128)S(1)}, u32[]{:S(2)}) copy-start(f32[96,4,64,128]{3,2,1,0:T(8,128)S(1)} %multiply_add_fusion) | copy-start | bytes 37748740
  70.2 14.8 %copy-start.8 = (f32[4]{0:T(128)S(1)}, f32[4]{0:T(128)}, u32[]{:S(2)}) copy-start(f32[4]{0:T(128)} %param.31) | copy-start | bytes 52
  70.2 46.4 %copy-start.12 = (bf16[256]{0:T(256)(128)(2,1)S(1)}, bf16[256]{0:T(256)(128)(2,1)}, u32[]{:S(2)}) copy-start(bf16[256]{0:T(256)(128)(2,1)} %param.32) | copy-start | bytes 1540
  84.8 33.5 %copy-start.6 = (s32[96,6]{0,1:T(8,128)S(1)}, s32[96,6]{0,1:T(8,128)}, u32[]{:S(2)}) copy-start(s32[96,6]{0,1:T(8,128)} %param.37) | copy-start | bytes 6916
  84.9 88.3 %copy-start.3 = (bf16[96,168]{0,1:T(8,128)(2,1)S(1)}, bf16[96,168]{0,1:T(8,128)(2,1)}, u32[]{:S(2)}) copy-start(bf16[96,168]{0,1:T(8,128)(2,1)} %param.20) | copy-start | bytes 96772
  253.7 18.4 %all-to-all-start.1 = ((bf16[16,2,8064]{2,1,0:T(2,128)(2,1)}), bf16[16,2,8064]{2,1,0:T(2,128)(2,1)}, u32[]{:S(2)}, u32[]{:S(2)}) async-start(bf16[16,2,8064]{2,1,0:T(2,128)(2,1)} %reshape.144), calls=%async_computation.1 | async-start | bytes 1032192 | tf_op jit(solution)/shard_map/all_to_all | solution.py:155
Sparse Core Ops, SparseCore 0:
  118.5 54.5 reduce-scatter.3
